TPU v7x, 256 devices: a whole 4x4x8 slice. The times are simulated.
256 devices in a mesh: row: 16 (over z, x_hi), col: 16 (over y, x_lo, core).
Axes of the slice: x: 4 (x_hi: 2, x_lo: 2; x = x_hi * 2 + x_lo), y: 4, z: 8, core: 2. Of those that a mesh axis runs over, the one named last changes fastest.
Arguments:
- front_base: float32 [8, 16, 128, 8, 16, 128], P(None, 'row', None, None, 'col')
- traces: bfloat16 [8, 16, 4, 3, 128, 128], P(None, 'row'), may hold values from -0.75 to 0.75
- adjacency: int32 [128, 4], replicated, may hold values from 0 to 127, as said below
- pivot_order: int32 [2, 512], replicated, may hold values from 0 to 511, each once within a row
- pivot_kind: int32 [2, 512], replicated, may hold values from 0 to 2, as said below
- inverse_diagonal: float32 [2, 512], replicated, may hold values from -0.3 to 0.3
- inverse_coupling: float32 [2, 512], replicated, may hold values from -0.3 to 0.3
- readers: int32 [2, 128], replicated, may hold values 0 or 1
Outputs:
- trailing: float32 [8, 16, 128, 8, 16, 128], P(None, 'row', None, None, 'col')
Inputs may be any that keep to these rules, and one draw needn't show every extreme that they name: The elements form a 16 x 8 grid that closes on itself in both dimensions, numbered in a drawn order; faces 0 and 1 lead to the next and previous element along the first dimension, 2 and 3 along the second, so adjacency[adjacency[e, f], f with its lowest bit flipped] = e. `pivot_kind`: 0 marks a 1 x 1 pivot; 1 marks the first position of a 2 x 2 pivot, whose second position follows and is marked 2; 2 x 2 pivots start at even positions.
All inputs are finite; a program needn't handle non-finite values.
Results may differ from a plain program's by a relative error of at most 0.008.
Values may be sent and summed in bfloat16 or wider, within the bound.
No kernel may reach another device: no remote copies, remote signals or barrier semaphores. Data moves between devices by JAX's collectives and lax.ppermute only.
A program may use at most 128 MiB of HBM per device.

v0:
```python
import jax
import jax.numpy as jnp
from jax import lax
from jax.sharding import PartitionSpec as P

NB = 128
PW = 512
PANELS = 2


def from_root(array, axis, root):
    mine = lax.axis_index(axis) == root
    return lax.psum(jnp.where(mine, array, jnp.zeros_like(array)), axis)


def face_left(values):
    return jnp.concatenate(
        [values[:, :, 0], values[:, :, 0], values[:, :, 1], values[:, :, 2]], axis=2
    )


def face_right(values):
    return jnp.concatenate(
        [
            4.0 * values[:, :, 0],
            -0.5 * values[:, :, 1],
            -0.5 * values[:, :, 0],
            2.0 * values[:, :, 2],
        ],
        axis=2,
    )


def apply_inverse(values, pivot_kinds, diagonal, pair_terms):
    starts = (pivot_kinds == 1).astype(values.dtype)
    upward = pair_terms * starts
    upward_prev = jnp.concatenate([jnp.zeros_like(upward[:1]), upward[:-1]])
    following = jnp.concatenate([values[:, 1:], jnp.zeros_like(values[:, :1])], axis=1)
    preceding = jnp.concatenate([jnp.zeros_like(values[:, :1]), values[:, :-1]], axis=1)
    return values * diagonal + following * upward + preceding * upward_prev


def local(
    front_base,
    traces,
    adjacency,
    pivot_order,
    pivot_kind,
    inverse_diagonal,
    inverse_coupling,
    readers,
):
    row_count = lax.axis_size("row")
    col_count = lax.axis_size("col")
    row_index = lax.axis_index("row")
    col_index = lax.axis_index("col")
    row_blocks = front_base.shape[0]
    col_blocks = front_base.shape[3]
    rows_total = row_blocks * NB
    local_traces = traces[:, 0]
    copy_index = 0
    received = [from_root(local_traces, "row", col_index + copy_index * col_count)]
    column_traces = jnp.stack(received, axis=1).reshape((col_blocks,) + local_traces.shape[1:])
    left_parts = face_left(local_traces)
    right_parts = face_right(local_traces)
    column_right = face_right(column_traces)
    opposite = jnp.array([1, 0, 3, 2], dtype=jnp.int32)
    local_elements = jnp.arange(row_blocks, dtype=jnp.int32) * row_count + row_index
    neighbour = jnp.take(adjacency, local_elements, axis=0)
    held_here = neighbour % col_count == col_index
    col_slot = neighbour // col_count
    partner = column_right[col_slot, opposite[None, :]]
    coupling = jnp.einsum(
        "efqi,efqj->efij", left_parts, partner, preferred_element_type=jnp.float32
    )
    self_terms = jnp.einsum(
        "efqi,efqj->eij", left_parts, right_parts, preferred_element_type=jnp.float32
    )
    slot_ids = jnp.arange(col_blocks, dtype=jnp.int32)
    place_pair = (held_here[:, :, None] & (col_slot[:, :, None] == slot_ids[None, None, :])).astype(
        jnp.float32
    )
    self_here = (local_elements % col_count == col_index)[:, None]
    place_self = (self_here & ((local_elements // col_count)[:, None] == slot_ids[None, :])).astype(
        jnp.float32
    )
    assembled = jnp.einsum("eij,ec->eicj", self_terms, place_self, precision=lax.Precision.HIGHEST)
    assembled = assembled - jnp.einsum(
        "efij,efc->eicj", coupling, place_pair, precision=lax.Precision.HIGHEST
    )
    front_mat = front_base.reshape(rows_total, col_blocks * NB) + assembled.reshape(
        rows_total, col_blocks * NB
    )
    panel_blocks = PW // NB
    for which_panel in range(PANELS):
        first_block = which_panel * panel_blocks
        front_slots = front_mat.reshape(rows_total, col_blocks, NB)
        low_slot = first_block // col_count
        high_slot = (first_block + panel_blocks - 1) // col_count
        slab_cols = front_slots[:, low_slot : high_slot + 1, :].astype(jnp.bfloat16)[:, :, None, :]
        gathered = lax.all_gather(slab_cols, "col", axis=2, tiled=True)
        gathered = gathered.reshape(rows_total, -1, NB)
        begin_block = first_block - low_slot * col_count
        columns = gathered[:, begin_block : begin_block + panel_blocks, :].reshape(rows_total, PW)
        columns = jnp.take(columns, pivot_order[which_panel], axis=1)
        kept_blocks = jnp.take(readers[which_panel], local_elements) * (
            local_elements >= first_block + panel_blocks
        ).astype(jnp.int32)
        kept_rows = jnp.repeat(kept_blocks, NB).astype(jnp.bfloat16)
        panel_vals = columns * kept_rows[:, None]
        scaled = apply_inverse(
            panel_vals.astype(jnp.float32),
            pivot_kind[which_panel],
            inverse_diagonal[which_panel],
            inverse_coupling[which_panel],
        ).astype(jnp.bfloat16)
        copy_index = 0
        incoming = from_root(panel_vals, "row", col_index + copy_index * col_count)
        transposed = [incoming.reshape(row_blocks, NB, PW)]
        col_panel = jnp.stack(transposed, axis=1).reshape(col_blocks * NB, PW)
        front_mat = front_mat - lax.dot_general(
            scaled, col_panel, (((1,), (1,)), ((), ())), preferred_element_type=jnp.float32
        )
    return front_mat.reshape(row_blocks, 1, NB, col_blocks, 1, NB)


def solution(mesh):
    in_specs = (
        P(None, "row", None, None, "col", None),
        P(None, "row", None, None, None, None),
        P(),
        P(),
        P(),
        P(),
        P(),
        P(),
    )
    out_specs = P(None, "row", None, None, "col", None)
    return jax.shard_map(local, mesh=mesh, in_specs=in_specs, out_specs=out_specs, check_vma=False)
```

profile of v0, /device:TPU:8, one launch (start us, length us, event | category | flops | bytes accessed | tf_op | source)
XLA Modules:
  0.0 654.4 jit_solution(11187019615183884576)
XLA Ops:
  6.5 3.8 broadcast_select_fusion
  10.3 0.0 all-reduce.8.cloned.1.call-update
  10.3 0.0 all-gather.5.cloned.1.call-start
  10.4 2.1 copy.69
  12.5 0.1 copy.33
  12.6 0.6 gather_fusion
  13.2 0.1 copy.34
  13.3 0.1 fusion.37
  13.4 0.1 copy.35
  13.5 0.1 reshape.311
  13.5 5.0 copy.39
  18.5 0.1 fusion.31
  18.6 0.1 fusion.29
  18.7 0.1 add_select_fusion
  18.8 0.4 slice_bitcast_fusion.2
  19.2 0.3 broadcast_multiply_fusion.3
  19.5 0.6 copy-done.1
  20.1 0.4 copy-done.3
  20.5 0.3 copy-done.5
  20.8 2.8 fusion.10
  23.6 169.1 %all-reduce.8.cloned.1.call-done = bf16[8,4,3,128,128]{4,3,1,0,2:T(8,128)(2,1)} async-done(((bf16[8,4,3,128,128]{4,3,1,0,2:T(8,128)(2,1)}), bf16[8,4,3,128,128]{4,3,1,0,2:T(8,128)(2,1)}) %all-reduce.8.cloned.1.call-update) | async-done | bytes 3145744 | tf_op jit(solution)/shard_map/psum | solution.py:13
  192.7 2.2 multiply_bitcast_fusion.1
  194.9 2.2 pad_maximum_fusion.1
  197.1 5.4 gather_fusion.1
  202.6 3.2 fusion.9
  205.8 4.5 multiply_subtract_fusion
  210.4 2.0 copy-done
  212.4 0.3 slice.139
  212.6 1.8 fusion.21
  214.5 0.0 all-gather.5.cloned.1.call-update
  214.5 0.0 all-reduce.10.cloned.1.call-start
  214.6 0.6 gather_fusion.3
  215.3 0.1 broadcast_bitcast_fusion.1
  215.4 36.0 %all-gather.5.cloned.1.call-done = bf16[1024,16,128]{2,0,1:T(8,128)(2,1)} async-done(((bf16[1024,1,128]{2,0,1:T(8,128)(2,1)}), bf16[1024,16,128]{2,0,1:T(8,128)(2,1)}) %all-gather.5.cloned.1.call-update) | async-done | bytes 4194320 | tf_op jit(solution)/shard_map/all_gather | solution.py:101
  251.4 1.3 slice.140
  252.7 0.5 copy.41
  253.2 2.1 gather_fusion.2
  255.3 1.3 fusion.47
  256.5 0.0 all-reduce.10.cloned.1.call-update
  256.6 0.2 all-gather.7.cloned.1.call-start
  256.8 5.2 copy.68
  262.0 5.4 copy.51
  267.4 0.1 pad_maximum_fusion.7
  267.5 5.3 copy.67
  272.8 5.5 copy.38
  278.2 2.4 fusion.50
  280.6 137.7 %all-reduce.10.cloned.1.call-done = bf16[1024,512]{0,1:T(8,128)(2,1)} async-done(((bf16[1024,512]{0,1:T(8,128)(2,1)}), bf16[1024,512]{0,1:T(8,128)(2,1)}) %all-reduce.10.cloned.1.call-update) | async-done | bytes 1048592 | tf_op jit(solution)/shard_map/psum | solution.py:13
  418.4 8.7 %fusion.53 = (bf16[1024,1024]{0,1:T(8,128)(2,1)S(1)}, f32[1024,1024]{0,1:T(8,128)}) fusion(bf16[1024,512]{0,1:T(8,128)(2,1)} %all-reduce.10.cloned.1.call-done, f32[1024,511]{0,1:T(8,128)} %get-tuple-element.21, f32[1024,511]{0,1:T(8,128)} %get-tuple-element.20, f32[512]{0:T(512)S(1)} %pad_maximum_fusion.7, f32[512]{0:T(512)S(1)} %bitcast.126, ...), kind=kOutput, calls=%fused_computation.126 | convolution fusion | flops 1081606144 | bytes 20972032 | tf_op jit(solution)/shard_map/dot_general | solution.py:121
  427.1 0.8 copy.52
  428.0 0.0 all-reduce.12.cloned.1.call-start
  428.0 0.6 gather_fusion.5
  428.7 0.1 broadcast_bitcast_fusion
  428.8 36.9 %all-gather.7.cloned.1.call-done = bf16[1024,16,128]{2,0,1:T(8,128)(2,1)} async-done(((bf16[1024,1,128]{2,0,1:T(8,128)(2,1)}), bf16[1024,16,128]{2,0,1:T(8,128)(2,1)}) %all-gather.7.cloned.1.call-update) | async-done | bytes 4194320 | tf_op jit(solution)/shard_map/all_gather | solution.py:101
  465.7 1.3 slice.145
  467.0 0.5 copy.43
  467.5 2.1 gather_fusion.4
  469.6 1.3 fusion.48
  470.9 0.0 all-reduce.12.cloned.1.call-update
  470.9 0.1 pad_maximum_fusion.6
  471.0 2.3 fusion.49
  473.3 159.0 %all-reduce.12.cloned.1.call-done = bf16[1024,512]{0,1:T(8,128)(2,1)} async-done(((bf16[1024,512]{0,1:T(8,128)(2,1)}), bf16[1024,512]{0,1:T(8,128)(2,1)}) %all-reduce.12.cloned.1.call-update) | async-done | bytes 1048592 | tf_op jit(solution)/shard_map/psum | solution.py:13
  632.3 5.5 subtract_bitcast_fusion
  637.7 3.0 copy.56
  640.7 7.2 %copy.45 = f32[8,1,128,8,1,128]{5,4,3,2,1,0:T(1,128)} copy(f32[8,1,128,8,1,128]{2,0,5,3,4,1:T(8,128)} %bitcast.118) | data formatting | bytes 8388608 | tf_op jit(solution)/shard_map/reshape | solution.py:124
  (46 shorter events, 0.2 us)
Async XLA Ops:
  6.5 186.2 %all-reduce.8.cloned.1.call-start = ((), (), s32[]{:S(2)}) async-start(), calls=%async_computation | async-start | bytes 6291456 | tf_op jit(solution)/shard_map/psum | solution.py:13
  10.3 2.2 copy-start.12
  10.3 3.0 copy-start.14
  10.3 241.0 %all-gather.5.cloned.1.call-start = ((), (), s32[]{:S(2)}) async-start(), calls=%async_computation.3 | async-start | bytes 4456448 | tf_op jit(solution)/shard_map/all_gather | solution.py:101
  19.1 1.0 copy-start.1
  19.2 1.3 copy-start.3
  19.2 1.7 copy-start.5
  197.1 5.4 copy-start.2
  197.1 5.4 copy-start.4
  197.1 5.4 copy-start.6
  202.6 3.2 copy-start.7
  205.8 8.8 %copy-start.13 = (s32[2,128]{1,0:T(2,128)S(1)}, s32[2,128]{1,0:T(2,128)}, u32[]{:S(2)}) copy-start(s32[2,128]{1,0:T(2,128)} %param.20) | copy-start | bytes 3076
  205.8 9.4 %copy-start.10 = (s32[2,512]{1,0:T(2,128)S(1)}, s32[2,512]{1,0:T(2,128)}, u32[]{:S(2)}) copy-start(s32[2,512]{1,0:T(2,128)} %param.16) | copy-start | bytes 12292
  210.4 2.0 copy-start
  214.5 203.9 %all-reduce.10.cloned.1.call-start = ((), (), s32[]{:S(2)}) async-start(), calls=%async_computation.1 | async-start | bytes 2097152 | tf_op jit(solution)/shard_map/psum | solution.py:13
  256.6 209.1 %all-gather.7.cloned.1.call-start = ((), (), s32[]{:S(2)}) async-start(), calls=%async_computation.4 | async-start | bytes 4456448 | tf_op jit(solution)/shard_map/all_gather | solution.py:101
  262.0 5.4 copy-start.8
  262.0 5.4 copy-start.9
  262.0 5.5 copy-start.11
  428.0 204.3 %all-reduce.12.cloned.1.call-start = ((), (), s32[]{:S(2)}) async-start(), calls=%async_computation.2 | async-start | bytes 2097152 | tf_op jit(solution)/shard_map/psum | solution.py:13
Sparse Core Ops, SparseCore 0:
  10.4 182.2 all-reduce.7
  214.6 36.6 all-gather.4
  256.7 161.6 all-reduce.9
  428.1 37.5 all-gather.6
  471.0 161.2 all-reduce.11
where the time goes:
time: 655 us; the launch traced here: 654 us
  waiting for transfers between devices  539 us (82%)
  local copies, waits for them, and re-layouts  63.8 us (10%)
  matrix products  24.7 us (4%)
  other arithmetic  13.4 us (2%)
  between operations  13.4 us (2%)
    psum x3, waiting for transfers between devices, from_root(): return lax.psum(jnp.where(mine, array, jnp.zeros_like(array)), axis)  466 us
    all_gather x2, waiting for transfers between devices, local(): gathered = lax.all_gather(slab_cols, 'col', axis=2, tiled=True)  72.9 us
    unnamed x37, local copies, waits for them, and re-layouts  24.8 us
    dot_general x2, matrix products, local(): lax.dot_general(scaled, col_panel, (((1,), (1,)), ((), ())), preferred_el...  14.2 us
  transfers between devices with their start and end apart: 5, of which 5 were waited for; matrix products, arithmetic and copies ran while one was open for 6% of the time, Pallas kernels for 0%

commit v1 on v0

--- a/solution.py
+++ b/solution.py
@@ -98,7 +98,8 @@
         low_slot = first_block // col_count
         high_slot = (first_block + panel_blocks - 1) // col_count
         slab_cols = front_slots[:, low_slot : high_slot + 1, :].astype(jnp.bfloat16)[:, :, None, :]
-        gathered = lax.all_gather(slab_cols, "col", axis=2, tiled=True)
+        sent = jnp.stack([slab_cols] * lax.axis_size("col"))
+        gathered = jnp.concatenate(lax.all_to_all(sent, "col", 0, 0), axis=2)
         gathered = gathered.reshape(rows_total, -1, NB)
         begin_block = first_block - low_slot * col_count
         columns = gathered[:, begin_block : begin_block + panel_blocks, :].reshape(rows_total, PW)

time: 655 us -> 686 us (1.047)
  waiting for transfers between devices: 539 us -> 556 us
  starting transfers between devices: 0.35 us -> 11.8 us
    all_to_all x0 -> x2, waiting for transfers between devices: none -> 95.7 us  [local(): gathered = jnp.concatenate(lax.all_to_all(sent, 'col', 0, 0), axis=2)]
    all_gather x2 -> x0, waiting for transfers between devices: 72.9 us -> none  [local(): gathered = lax.all_gather(slab_cols, 'col', axis=2, tiled=True)]
    all_to_all x0 -> x2, starting transfers between devices: none -> 11.5 us  [local(): gathered = jnp.concatenate(lax.all_to_all(sent, 'col', 0, 0), axis=2)]
    unnamed x37 -> x36, local copies, waits for them, and re-layouts: 24.8 us -> 23.9 us
where the time goes in v1:
time: 686 us
  waiting for transfers between devices  556 us (81%)
  local copies, waits for them, and re-layouts  67 us (10%)
  matrix products  24.7 us (4%)
  between operations  13.4 us (2%)
  other arithmetic  12.8 us (2%)
  starting transfers between devices  11.8 us (2%)
    psum x3, waiting for transfers between devices, from_root(): return lax.psum(jnp.where(mine, array, jnp.zeros_like(array)), axis)  460 us
    all_to_all x2, waiting for transfers between devices, local(): gathered = jnp.concatenate(lax.all_to_all(sent, 'col', 0, 0), axis=2)  95.7 us
    unnamed x36, local copies, waits for them, and re-layouts  23.9 us
    dot_general x2, matrix products, local(): lax.dot_general(scaled, col_panel, (((1,), (1,)), ((), ())), preferred_el...  14.2 us
  transfers between devices with their start and end apart: 5, of which 5 were waited for; matrix products, arithmetic and copies ran while one was open for 6% of the time, Pallas kernels for 0%

profile of v1, /device:TPU:8, one launch (start us, length us, event | category | flops | bytes accessed | tf_op | source)
XLA Modules:
  0.0 685.6 jit_solution(3744273869198161678)
XLA Ops:
  6.5 3.8 broadcast_select_fusion
  10.3 0.0 all-reduce.8.cloned.1.call-update
  10.3 2.1 copy.70
  12.5 0.1 copy.35
  12.6 0.6 gather_fusion
  13.1 0.1 copy.36
  13.2 0.0 copy-done.14
  13.2 0.1 fusion.38
  13.3 0.1 copy.37
  13.4 0.1 reshape.317
  13.5 5.0 copy.41
  18.5 0.1 fusion.32
  18.5 0.1 fusion.30
  18.6 0.1 add_select_fusion
  18.7 0.4 slice_bitcast_fusion.2
  19.1 0.3 broadcast_multiply_fusion.3
  19.5 0.6 copy-done.1
  20.1 0.4 copy-done.3
  20.4 0.3 copy-done.5
  20.8 2.8 fusion.10
  23.5 169.3 %all-reduce.8.cloned.1.call-done = bf16[8,4,3,128,128]{4,3,1,0,2:T(8,128)(2,1)} async-done(((bf16[8,4,3,128,128]{4,3,1,0,2:T(8,128)(2,1)}), bf16[8,4,3,128,128]{4,3,1,0,2:T(8,128)(2,1)}) %all-reduce.8.cloned.1.call-update) | async-done | bytes 3145744 | tf_op jit(solution)/shard_map/psum | solution.py:13
  192.8 2.2 multiply_bitcast_fusion.1
  195.0 2.2 pad_maximum_fusion.1
  197.2 5.4 gather_fusion.1
  202.7 3.2 fusion.9
  205.9 4.5 multiply_subtract_fusion
  210.5 2.0 copy-done
  212.5 0.3 slice.139
  212.8 1.1 fusion.24
  213.9 0.1 copy.43
  214.1 2.5 stack.6
  216.6 6.1 all-to-all-start
  222.7 0.2 all-reduce.10.cloned.1.call-start
  223.0 0.6 gather_fusion.3
  223.7 0.1 broadcast_bitcast_fusion.1
  223.8 47.7 %all-to-all-done = bf16[16,1024,1,1,128]{1,4,3,2,0:T(8,128)(2,1)} async-done(((bf16[16,1024,1,1,128]{1,4,3,2,0:T(8,128)(2,1)}), bf16[16,1024,1,1,128]{1,4,3,2,0:T(8,128)(2,1)}, u32[]{:S(2)}, u32[]{:S(2)}) %all-to-all-start) | async-done | bytes 4194336 | tf_op jit(solution)/shard_map/all_to_all | solution.py:102
  271.5 1.3 slice.140
  272.8 2.1 gather_fusion.2
  274.9 1.3 fusion.48
  276.1 0.0 all-reduce.10.cloned.1.call-update
  276.2 5.2 copy.69
  281.4 5.4 copy.51
  286.8 0.1 pad_maximum_fusion.7
  286.9 5.2 copy.68
  292.1 5.5 copy.40
  297.6 2.4 fusion.51
  300.0 134.3 %all-reduce.10.cloned.1.call-done = bf16[1024,512]{0,1:T(8,128)(2,1)} async-done(((bf16[1024,512]{0,1:T(8,128)(2,1)}), bf16[1024,512]{0,1:T(8,128)(2,1)}) %all-reduce.10.cloned.1.call-update) | async-done | bytes 1048592 | tf_op jit(solution)/shard_map/psum | solution.py:13
  434.2 8.7 %fusion.54 = (bf16[1024,1024]{0,1:T(8,128)(2,1)S(1)}, f32[1024,1024]{0,1:T(8,128)}) fusion(bf16[1024,512]{0,1:T(8,128)(2,1)} %all-reduce.10.cloned.1.call-done, f32[1024,511]{0,1:T(8,128)} %get-tuple-element.21, f32[1024,511]{0,1:T(8,128)} %get-tuple-element.20, f32[512]{0:T(512)S(1)} %pad_maximum_fusion.7, f32[512]{0:T(512)S(1)} %bitcast.136, ...), kind=kOutput, calls=%fused_computation.128 | convolution fusion | flops 1081606144 | bytes 20972032 | tf_op jit(solution)/shard_map/dot_general | solution.py:122
  443.0 2.6 stack.7
  445.6 5.4 all-to-all-start.1
  451.0 0.0 all-reduce.12.cloned.1.call-start
  451.0 0.6 gather_fusion.5
  451.7 0.1 broadcast_bitcast_fusion
  451.8 48.0 %all-to-all-done.1 = bf16[16,1024,1,1,128]{1,4,3,2,0:T(8,128)(2,1)} async-done(((bf16[16,1024,1,1,128]{1,4,3,2,0:T(8,128)(2,1)}), bf16[16,1024,1,1,128]{1,4,3,2,0:T(8,128)(2,1)}, u32[]{:S(2)}, u32[]{:S(2)}) %all-to-all-start.1) | async-done | bytes 4194336 | tf_op jit(solution)/shard_map/all_to_all | solution.py:102
  499.8 1.3 slice.145
  501.1 2.1 gather_fusion.4
  503.1 1.3 fusion.49
  504.4 0.0 all-reduce.12.cloned.1.call-update
  504.4 0.1 pad_maximum_fusion.6
  504.5 2.3 fusion.50
  506.8 156.6 %all-reduce.12.cloned.1.call-done = bf16[1024,512]{0,1:T(8,128)(2,1)} async-done(((bf16[1024,512]{0,1:T(8,128)(2,1)}), bf16[1024,512]{0,1:T(8,128)(2,1)}) %all-reduce.12.cloned.1.call-update) | async-done | bytes 1048592 | tf_op jit(solution)/shard_map/psum | solution.py:13
  663.5 5.5 subtract_bitcast_fusion
  668.9 3.0 copy.55
  671.9 7.2 %copy.45 = f32[8,1,128,8,1,128]{5,4,3,2,1,0:T(1,128)} copy(f32[8,1,128,8,1,128]{2,0,5,3,4,1:T(8,128)} %bitcast.128) | data formatting | bytes 8388608 | tf_op jit(solution)/shard_map/reshape | solution.py:125
  (44 shorter events, 0.2 us)
Async XLA Ops:
  6.5 186.3 %all-reduce.8.cloned.1.call-start = ((), (), s32[]{:S(2)}) async-start(), calls=%async_computation.2 | async-start | bytes 6291456 | tf_op jit(solution)/shard_map/psum | solution.py:13
  10.3 2.2 copy-start.12
  10.3 2.9 copy-start.14
  19.1 1.0 copy-start.1
  19.1 1.3 copy-start.3
  19.1 1.7 copy-start.5
  197.2 5.5 copy-start.2
  197.2 5.5 copy-start.4
  197.2 5.5 copy-start.6
  202.7 3.2 copy-start.7
  210.5 2.0 copy-start
  216.6 6.4 copy-start.13
  216.6 7.0 %copy-start.10 = (s32[2,512]{1,0:T(2,128)S(1)}, s32[2,512]{1,0:T(2,128)}, u32[]{:S(2)}) copy-start(s32[2,512]{1,0:T(2,128)} %param.16) | copy-start | bytes 12292
  216.6 54.9 %all-to-all-start = ((bf16[16,1024,1,1,128]{1,4,3,2,0:T(8,128)(2,1)}), bf16[16,1024,1,1,128]{1,4,3,2,0:T(8,128)(2,1)}, u32[]{:S(2)}, u32[]{:S(2)}) async-start(bf16[16,1024,1,1,128]{1,4,3,2,0:T(8,128)(2,1)} %stack.6), calls=%async_computation | async-start | bytes 8388608 | tf_op jit(solution)/shard_map/all_to_all | solution.py:102
  222.7 211.5 %all-reduce.10.cloned.1.call-start = ((), (), s32[]{:S(2)}) async-start(), calls=%async_computation.3 | async-start | bytes 2097152 | tf_op jit(solution)/shard_map/psum | solution.py:13
  281.4 5.4 copy-start.8
  281.4 5.4 copy-start.9
  281.4 5.5 copy-start.11
  445.6 54.2 %all-to-all-start.1 = ((bf16[16,1024,1,1,128]{1,4,3,2,0:T(8,128)(2,1)}), bf16[16,1024,1,1,128]{1,4,3,2,0:T(8,128)(2,1)}, u32[]{:S(2)}, u32[]{:S(2)}) async-start(bf16[16,1024,1,1,128]{1,4,3,2,0:T(8,128)(2,1)} %stack.7), calls=%async_computation.1 | async-start | bytes 8388608 | tf_op jit(solution)/shard_map/all_to_all | solution.py:102
  451.0 212.5 %all-reduce.12.cloned.1.call-start = ((), (), s32[]{:S(2)}) async-start(), calls=%async_computation.4 | async-start | bytes 2097152 | tf_op jit(solution)/shard_map/psum | solution.py:13
Sparse Core Ops, SparseCore 0:
  10.4 182.3 all-reduce.7
  276.3 157.9 all-reduce.9
  504.5 158.8 all-reduce.11
